TPU v7x, 128 devices: a whole 4x4x4 slice. The times are simulated.
128 devices in a mesh: dp: 8 (over x_lo, y), expert: 16 (over x_hi, z, core).
Axes of the slice: x: 4 (x_hi: 2, x_lo: 2; x = x_hi * 2 + x_lo), y: 4, z: 4, core: 2. Of those that a mesh axis runs over, the one named last changes fastest.
Arguments:
- tokens: bfloat16 [65536, 2048], P(('dp', 'expert')), may hold values from -6 to 6
- probe: bfloat16 [65536, 2048], P(('dp', 'expert')), may hold values from -20 to 20
- domain: int32 [65536], P(('dp', 'expert')), may hold values from 0 to 21
- mix: float32 [22], replicated, may hold values from 0.5 to 2
- router: bfloat16 [2048, 32], replicated, may hold values from -0.125 to 0.125
- picks: int32 [128, 32, 40], P(('dp', 'expert')), may hold values from 0 to 511, as said below
- w_gate: bfloat16 [2048, 32, 768], P(None, 'expert'), may hold values from -0.125 to 0.125
- w_up: bfloat16 [2048, 32, 768], P(None, 'expert'), may hold values from -0.125 to 0.125
- w_down: bfloat16 [2048, 32, 768], P(None, 'expert'), may hold values from -0.21875 to 0.21875
Outputs:
- domain_loss: float32 [22], replicated
- router_grad: float32 [2048, 32], replicated
- grad_gate: bfloat16 [2048, 32, 768], P('dp', 'expert')
- grad_up: bfloat16 [2048, 32, 768], P('dp', 'expert')
- grad_down: bfloat16 [2048, 32, 768], P('dp', 'expert')
Inputs may be any that keep to these rules, and one draw needn't show every extreme that they name: The 40 picks of one expert on one device are distinct token positions of that device.
All inputs are finite; a program needn't handle non-finite values.
Results may differ from a plain program's by a relative error of at most 0.018.
Values may be sent and summed in bfloat16 or wider, within the bound.
A program may use at most 192 MiB of HBM per device.

v0:
```python
import math
import jax
import jax.numpy as jnp
from jax import lax
from jax.sharding import PartitionSpec as P


def body(tokens, probe, domain, mix, router, picks, w_gate, w_up, w_down):
    token_count, model_width = tokens.shape
    expert_count = router.shape[1]
    slot_count = picks.shape[2]
    domain_count = mix.shape[0]
    data_devices = lax.axis_size("dp")
    expert_devices = lax.axis_size("expert")
    chosen = picks[0]
    logits = jnp.dot(tokens, router, preferred_element_type=jnp.float32)
    gate_vals = jax.nn.sigmoid(jnp.take_along_axis(logits.T, chosen, axis=1))
    outgoing = tokens[chosen].reshape(expert_count, 1, slot_count, model_width)
    received = lax.all_to_all(outgoing, "expert", split_axis=0, concat_axis=1, tiled=True)
    pre_gate = jnp.einsum("jsrd,djf->jsrf", received, w_gate, preferred_element_type=jnp.float32)
    pre_up = jnp.einsum("jsrd,djf->jsrf", received, w_up, preferred_element_type=jnp.float32)
    expert_hidden = (jax.nn.silu(pre_gate) * pre_up).astype(jnp.bfloat16)
    result = jnp.einsum(
        "jsrf,djf->jsrd", expert_hidden, w_down, preferred_element_type=jnp.float32
    ).astype(jnp.bfloat16)
    returned = lax.all_to_all(result, "expert", split_axis=1, concat_axis=0, tiled=True)
    returned, arrived, pre_gate, pre_up, hidden = (
        returned,
        received,
        pre_gate,
        pre_up,
        expert_hidden,
    )
    outputs = returned.reshape(expert_count, slot_count, model_width).astype(jnp.float32)
    contrib = gate_vals[:, :, None] * outputs
    flat_index = chosen.reshape(-1)
    added = (
        jnp.zeros((token_count, model_width), jnp.float32)
        .at[flat_index]
        .add(contrib.reshape(-1, model_width))
    )
    layer_out = tokens.astype(jnp.float32) + added
    difference = layer_out - probe.astype(jnp.float32)
    per_token = jnp.sum(difference * difference, axis=1)
    member = (domain[:, None] == jnp.arange(domain_count, dtype=jnp.int32)[None, :]).astype(
        jnp.float32
    )
    local_loss = jnp.sum(per_token[:, None] * member, axis=0)
    loss_total = lax.psum(local_loss, ("dp", "expert"))
    total_tokens = token_count * data_devices * expert_devices
    loss_scale = 1.0 / math.sqrt(data_devices * expert_devices * slot_count)
    weight_tok = jnp.sum(member * mix[None, :], axis=1)
    upstream = (loss_scale * weight_tok)[:, None] * difference
    picked_up = upstream[chosen]
    gate_slope = jnp.sum(picked_up * outputs, axis=2)
    logit_grad = gate_slope * gate_vals * (1.0 - gate_vals)
    expert_ids = jnp.broadcast_to(jnp.arange(expert_count, dtype=jnp.int32)[:, None], chosen.shape)
    placed = (
        jnp.zeros((token_count, expert_count), jnp.float32).at[chosen, expert_ids].set(logit_grad)
    )
    router_part = jnp.dot(tokens.astype(jnp.float32).T, placed, precision=lax.Precision.HIGHEST)
    sending = (
        (gate_vals[:, :, None] * picked_up)
        .astype(jnp.bfloat16)
        .reshape(expert_count, 1, slot_count, model_width)
    )
    back_grad = lax.all_to_all(sending, "expert", split_axis=0, concat_axis=1, tiled=True)
    hidden_grad = jnp.einsum(
        "jsrd,djf->jsrf", back_grad, w_down, preferred_element_type=jnp.float32
    )
    sigmoid_gate = jax.nn.sigmoid(pre_gate)
    gate_in = (
        hidden_grad * pre_up * sigmoid_gate * (1.0 + pre_gate * (1.0 - sigmoid_gate))
    ).astype(jnp.bfloat16)
    up_in = (hidden_grad * jax.nn.silu(pre_gate)).astype(jnp.bfloat16)

    def input_term(grads_in):
        return jnp.einsum("jsrd,jsrf->djf", arrived, grads_in, preferred_element_type=jnp.float32)

    grad_gate = lax.psum_scatter(
        input_term(gate_in).astype(jnp.bfloat16), "dp", scatter_dimension=0, tiled=True
    )
    grad_up = lax.psum_scatter(
        input_term(up_in).astype(jnp.bfloat16), "dp", scatter_dimension=0, tiled=True
    )
    grad_down = lax.psum_scatter(
        jnp.einsum("jsrd,jsrf->djf", back_grad, hidden, preferred_element_type=jnp.float32).astype(
            jnp.bfloat16
        ),
        "dp",
        scatter_dimension=0,
        tiled=True,
    )
    router_total = lax.psum(router_part, ("dp", "expert"))
    domain_loss = loss_total * (domain_count / (total_tokens * model_width))
    return (domain_loss, router_total, grad_gate, grad_up, grad_down)


def solution(mesh):
    placed = (
        P(("dp", "expert"), None),
        P(("dp", "expert"), None),
        P(("dp", "expert")),
        P(),
        P(),
        P(("dp", "expert"), None, None),
        P(None, "expert", None),
        P(None, "expert", None),
        P(None, "expert", None),
    )
    return jax.shard_map(
        body,
        mesh=mesh,
        in_specs=placed,
        out_specs=(
            P(),
            P(),
            P("dp", "expert", None),
            P("dp", "expert", None),
            P("dp", "expert", None),
        ),
        check_vma=False,
    )
```

profile of v0, /device:TPU:1, one launch (start us, length us, event | category | flops | bytes accessed | tf_op | source)
XLA Modules:
  0.0 717.0 jit_solution(11860185707785233741)
XLA Ops:
  8.9 12.7 %gather_fusion = bf16[1280,2048]{1,0:T(8,128)(2,1)} fusion(bf16[512,2048]{1,0:T(8,128)(2,1)} %param.9, s32[2048]{0:T(1024)S(1)} %pad_clamp_fusion), kind=kCustom, calls=%fused_computation | custom fusion | bytes 10490880 | tf_op jit(solution)/shard_map/gather | solution.py:18
  21.6 71.7 %all_to_all.45 = bf16[32,1,40,2048]{3,2,1,0:T(8,128)(2,1)S(1)} all-to-all(bf16[32,1,40,2048]{3,2,1,0:T(8,128)(2,1)} %bitcast.90), channel_id=1, replica_groups=mesh['dp'=8,'expert'=16] {'expert'}, dimensions={0} | all-to-all | bytes 10485760 | tf_op jit(solution)/shard_map/all_to_all | solution.py:19
  93.3 4.4 fusion.6
  97.7 6.5 multiply_convert_fusion.3
  104.3 7.7 %fusion.20 = bf16[2,16,40,2048]{3,2,1,0:T(8,128)(2,1)S(1)} fusion(bf16[2,16,40,768]{3,2,1,0:T(8,128)(2,1)} %get-tuple-element.36, bf16[2048,2,768,1]{2,1,0,3:T(2,128)(2,1)} %bitcast.102), kind=kOutput, calls=%fused_computation.34 | convolution fusion | flops 4029153280 | bytes 13500416 | tf_op jit(solution)/shard_map/jsrf,djf->jsrd/dot_general | solution.py:23
  114.7 5.6 all-to-all-start.1
  124.4 10.1 %gather_fusion.2 = f32[1280]{0:T(1024)S(1)} fusion(f32[32,512]{1,0:T(8,128)S(1)} %fusion.36, s32[1280]{0:T(1024)S(1)} %reshape.165), kind=kCustom, calls=%fused_computation.2 | custom fusion | bytes 20480 | tf_op jit(solution)/shard_map/jit(take_along_axis)/gather | solution.py:17
  134.7 55.0 %all-to-all-done.1 = bf16[2,16,40,2048]{3,2,0,1:T(8,128)(2,1)} async-done(((bf16[2,16,40,2048]{3,2,0,1:T(8,128)(2,1)}), bf16[2,16,40,2048]{3,2,0,1:T(8,128)(2,1)}, u32[]{:S(2)}, u32[]{:S(2)}) %all-to-all-start.1) | async-done | bytes 5242912 | tf_op jit(solution)/shard_map/all_to_all | solution.py:26
  189.7 3.9 bitcast_convert_fusion.3
  193.5 4.6 bitcast_multiply_fusion
  198.2 25.3 %scatter_fusion = f32[512,2048]{1,0:T(8,128)} fusion(f32[512,2048]{1,0:T(8,128)} %convert_element_type.66, s32[1280]{0:T(1024)S(1)} %fusion.33, f32[1280,2048]{1,0:T(8,128)} %bitcast_multiply_fusion), kind=kCustom, calls=%fused_computation.3 | custom fusion | flops 2621440 | bytes 31462400 | tf_op jit(solution)/shard_map/scatter-add | solution.py:40
  229.5 13.0 %gather_fusion.1 = f32[1280,2048]{1,0:T(8,128)} fusion(f32[512,2048]{1,0:T(8,128)} %fusion.28, s32[2048]{0:T(1024)S(1)} %pad_clamp_fusion), kind=kCustom, calls=%fused_computation.1 | custom fusion | bytes 20976640 | tf_op jit(solution)/shard_map/gather | solution.py:54
  242.5 6.7 fusion
  253.9 76.7 %all_to_all.46 = bf16[32,1,40,2048]{3,2,1,0:T(8,128)(2,1)S(1)} all-to-all(bf16[32,1,40,2048]{3,2,1,0:T(8,128)(2,1)} %multiply_convert_fusion), channel_id=1, replica_groups=mesh['dp'=8,'expert'=16] {'expert'}, dimensions={0} | all-to-all | bytes 10485760 | tf_op jit(solution)/shard_map/all_to_all | solution.py:67
  332.8 7.1 fusion.3
  340.2 8.2 %fusion.8 = f32[2,16,40,768]{3,2,1,0:T(8,128)S(1)} fusion(bf16[2048,2,768,1]{2,1,0,3:T(2,128)(2,1)} %bitcast.103, bf16[16,2,1,40,2048]{4,3,1,0,2:T(8,128)(2,1)} %bitcast.96), kind=kOutput, calls=%fused_computation.19 | convolution fusion | flops 4026531840 | bytes 15466496 | tf_op jit(solution)/shard_map/jsrd,djf->jsrf/dot_general | solution.py:68
  350.4 9.9 %fusion.2 = bf16[2048,2,768]{0,2,1:T(8,128)(2,1)} fusion(bf16[16,2,1,40,2048]{4,3,1,0,2:T(8,128)(2,1)} %bitcast.93, f32[2,16,40,768]{3,2,1,0:T(8,128)S(1)} %fusion.8, f32[2,16,40,768]{3,2,1,0:T(8,128)S(1)} %copy-done.18), kind=kOutput, calls=%fused_computation.13 | convolution fusion | flops 4035575808 | bytes 19398656 | tf_op jit(solution)/shard_map/jsrd,jsrf->djf/dot_general | solution.py:78
  360.3 12.5 %fusion.1 = bf16[2048,2,768]{0,2,1:T(8,128)(2,1)} fusion(bf16[16,2,1,40,2048]{4,3,1,0,2:T(8,128)(2,1)} %bitcast.94, f32[2,16,40,768]{3,2,1,0:T(8,128)} %copy-done.17, f32[2,16,40,768]{3,2,1,0:T(8,128)} %copy-done.19, f32[2,16,40,768]{3,2,1,0:T(8,128)} %get-tuple-element.37), kind=kOutput, calls=%fused_computation.12 | convolution fusion | flops 4039507968 | bytes 23330816 | tf_op jit(solution)/shard_map/jsrd,jsrf->djf/dot_general | solution.py:78
  373.8 187.1 %psum.14 = f32[22]{0:T(128)S(1)} all-reduce(f32[22]{0:T(128)S(1)} %get-tuple-element.31), channel_id=1, replica_groups=mesh['dp'=8,'expert'=16] {'dp','expert'}, use_global_device_ids=true, to_apply=%region_3.4 | all-reduce | flops 22 | bytes 176 | tf_op jit(solution)/shard_map/psum | solution.py:49
  561.0 5.3 scatter_custom_fusion.1
  568.7 3.0 copy.72
  571.7 3.0 copy.71
  574.8 3.0 copy.70
  577.8 130.2 %all-reduce.2.cloned.1.call-done = f32[2048,32]{0,1:T(8,128)} async-done(((f32[2048,32]{0,1:T(8,128)}), f32[2048,32]{0,1:T(8,128)}) %all-reduce.2.cloned.1.call-update) | async-done | bytes 262160 | tf_op jit(solution)/shard_map/psum | solution.py:94
  (86 shorter events, 27.9 us)
Async XLA Ops:
  8.0 115.7 %copy-start = (bf16[2048,32]{0,1:T(8,128)(2,1)S(1)}, bf16[2048,32]{0,1:T(8,128)(2,1)}, u32[]{:S(2)}) copy-start(bf16[2048,32]{0,1:T(8,128)(2,1)} %param.13) | copy-start | bytes 393220
  8.8 12.8 %copy-start.10 = (s32[32,40,1]{1,0,2:T(8,128)}, s32[32,40,1]{1,0,2:T(8,128)S(1)}, u32[]{:S(2)}) copy-start(s32[32,40,1]{1,0,2:T(8,128)S(1)} %get-tuple-element.35) | copy-start | bytes 15364
  21.6 71.7 %copy-start.16 = (bf16[2048,2,768]{2,1,0:T(2,128)(2,1)S(1)}, bf16[2048,2,768]{2,1,0:T(2,128)(2,1)}, u32[]{:S(2)}) copy-start(bf16[2048,2,768]{2,1,0:T(2,128)(2,1)} %param.15) | copy-start | bytes 18874372
  21.6 76.1 %slice-start = ((s8[6291456]{0:T(1024)(128)(4,1)}), s8[4194304]{0:T(1024)(128)(4,1)S(1)}, s32[]{:S(2)}) async-start(s8[6291456]{0:T(1024)(128)(4,1)} %bitcast.99), calls=%async_computation.10 | async-start | bytes 8388608
  93.3 4.4 copy-start.7
  93.3 4.4 slice-start.1
  97.7 6.6 copy-start.17
  114.7 6.2 copy-start.9
  114.7 6.3 copy-start.3
  114.7 75.0 %all-to-all-start.1 = ((bf16[2,16,40,2048]{3,2,0,1:T(8,128)(2,1)}), bf16[2,16,40,2048]{3,2,0,1:T(8,128)(2,1)}, u32[]{:S(2)}, u32[]{:S(2)}) async-start(bf16[2,16,40,2048]{3,2,0,1:T(8,128)(2,1)} %copy.64), calls=%async_computation.1 | async-start | bytes 10485760 | tf_op jit(solution)/shard_map/all_to_all | solution.py:26
  120.3 448.4 %reduce-scatter.8.cloned.1.call-start = ((), (), s32[]{:S(2)}) async-start(), calls=%async_computation.9 | async-start | bytes 7077888 | tf_op jit(solution)/shard_map/reduce_scatter | solution.py:86
  198.2 25.3 %copy-start.6 = (bf16[512,2048]{1,0:T(8,128)(2,1)S(1)}, bf16[512,2048]{1,0:T(8,128)(2,1)}, u32[]{:S(2)}) copy-start(bf16[512,2048]{1,0:T(8,128)(2,1)} %param.10) | copy-start | bytes 6291460
  223.5 3.0 copy-start.12
  223.6 3.0 copy-start.15
  223.6 3.5 copy-start.2
  242.5 8.5 %copy-start.5 = (f32[1280,2048]{1,0:T(8,128)S(1)}, f32[1280,2048]{1,0:T(8,128)}, u32[]{:S(2)}) copy-start(f32[1280,2048]{1,0:T(8,128)} %gather_fusion.1) | copy-start | bytes 31457284
  253.9 79.0 %copy-start.20 = (bf16[2,16,40,768]{3,2,1,0:T(8,128)(2,1)S(1)}, bf16[2,16,40,768]{3,2,1,0:T(8,128)(2,1)}, u32[]{:S(2)}) copy-start(bf16[2,16,40,768]{3,2,1,0:T(8,128)(2,1)} %get-tuple-element.36) | copy-start | bytes 5898244
  330.5 2.3 copy-start.8
  340.0 231.8 %reduce-scatter.6.cloned.1.call-start = ((), (), s32[]{:S(2)}) async-start(), calls=%async_computation.8 | async-start | bytes 7077888 | tf_op jit(solution)/shard_map/reduce_scatter | solution.py:83
  340.2 10.1 %copy-start.18 = (f32[2,16,40,768]{3,2,1,0:T(8,128)S(1)}, f32[2,16,40,768]{3,2,1,0:T(8,128)}, u32[]{:S(2)}) copy-start(f32[2,16,40,768]{3,2,1,0:T(8,128)} %copy-done.17) | copy-start | bytes 11796484
  360.3 214.5 %reduce-scatter.4.cloned.1.call-start = ((), (), s32[]{:S(2)}) async-start(), calls=%async_computation.7 | async-start | bytes 7077888 | tf_op jit(solution)/shard_map/reduce_scatter | solution.py:80
  372.8 193.5 %copy-start.4 = (bf16[512,2048]{1,0:T(8,128)(2,1)S(1)}, bf16[512,2048]{1,0:T(8,128)(2,1)}, u32[]{:S(2)}) copy-start(bf16[512,2048]{1,0:T(8,128)(2,1)} %param.9) | copy-start | bytes 6291460
  372.8 336.8 %copy-start.1 = (bf16[2048,32]{0,1:T(8,128)(2,1)S(1)}, bf16[2048,32]{0,1:T(8,128)(2,1)}, u32[]{:S(2)}) copy-start(bf16[2048,32]{0,1:T(8,128)(2,1)} %param.13) | copy-start | bytes 393220
  372.9 335.1 %all-reduce.2.cloned.1.call-start = ((), (), s32[]{:S(2)}) async-start(), calls=%async_computation.6 | async-start | bytes 524288 | tf_op jit(solution)/shard_map/psum | solution.py:94
  (4 other events, 4.2 us)
Sparse Core Ops, SparseCore 0:
  340.1 71.2 reduce-scatter.7
  413.8 71.8 reduce-scatter.5
  488.1 72.0 reduce-scatter.3
Sparse Core Ops, SparseCore 1:
  568.3 139.7 all-reduce.1
where the time goes:
time: 720 us; the launch traced here: 717 us
  blocking collectives  336 us (47%)
  waiting for transfers between devices  185 us (26%)
  local copies, waits for them, and re-layouts  62.2 us (9%)
  matrix products  58.8 us (8%)
  other arithmetic  53 us (7%)
  between operations  15.7 us (2%)
    psum x1, blocking collectives, body(): loss_total = lax.psum(local_loss, ('dp', 'expert'))  187 us
    psum x1, waiting for transfers between devices, body(): router_total = lax.psum(router_part, ('dp', 'expert'))  130 us
    all_to_all x1, blocking collectives, body(): lax.all_to_all(sending, 'expert', split_axis=0, concat_axis=1, tiled=True)  76.7 us
    all_to_all x1, blocking collectives, body(): lax.all_to_all(outgoing, 'expert', split_axis=0, concat_axis=1, tiled=True)  71.7 us
    all_to_all x1, waiting for transfers between devices, body(): lax.all_to_all(result, 'expert', split_axis=1, concat_axis=0, tiled=True)  55 us
    scatter-add x1, other arithmetic, body(): added = jnp.zeros((token_count, model_width), jnp.float32).at[flat_index]...  25.3 us
    unnamed x53, local copies, waits for them, and re-layouts  23.1 us
    dot_general x2, matrix products, input_term(): jnp.einsum('jsrd,jsrf->djf', arrived, grads_in, preferred_element_type=jn...  22.4 us
  transfers between devices with their start and end apart: 5, of which 2 were waited for; matrix products, arithmetic and copies ran while one was open for 9% of the time, Pallas kernels for 0%

commit v1 on v0

--- a/solution.py
+++ b/solution.py
@@ -91,7 +91,7 @@
         scatter_dimension=0,
         tiled=True,
     )
-    router_total = lax.psum(router_part, ("dp", "expert"))
+    router_total = lax.psum(lax.psum(router_part, "expert"), axis_name="dp")
     domain_loss = loss_total * (domain_count / (total_tokens * model_width))
     return (domain_loss, router_total, grad_gate, grad_up, grad_down)
 

time: 720 us -> 669 us (0.929)
  blocking collectives: 336 us -> 223 us
  waiting for transfers between devices: 185 us -> 225 us
  starting transfers between devices: 6.54 us -> 21.6 us
    all_to_all x1 -> x0, blocking collectives: 76.7 us -> none  [body(): lax.all_to_all(sending, 'expert', split_axis=0, concat_axis=1, tiled=True)]
    all_to_all x0 -> x1, waiting for transfers between devices: none -> 64.7 us  [body(): lax.all_to_all(sending, 'expert', split_axis=0, concat_axis=1, tiled=True)]
    psum x1, blocking collectives: 187 us -> 152 us  [body(): loss_total = lax.psum(local_loss, ('dp', 'expert'))]
    psum x1 -> x2, waiting for transfers between devices: 130 us -> 105 us  [body(): router_total = lax.psum(lax.psum(router_part, 'expert'), axis_name='dp')]
    all_to_all x0 -> x1, starting transfers between devices: none -> 14.8 us  [body(): lax.all_to_all(sending, 'expert', split_axis=0, concat_axis=1, tiled=True)]
    unnamed x53 -> x47, local copies, waits for them, and re-layouts: 23.1 us -> 20.9 us
  transfers between devices with their start and end apart: 5 -> 7, of which waited for: 2 -> 4; matrix products, arithmetic and copies ran while one was open for 9% -> 11% of each run, Pallas kernels for 0% -> 0%
where the time goes in v1:
time: 669 us; the launch traced here: 661 us
  waiting for transfers between devices  225 us (34%)
  blocking collectives  223 us (33%)
  matrix products  61.2 us (9%)
  local copies, waits for them, and re-layouts  59.9 us (9%)
  other arithmetic  54 us (8%)
  starting transfers between devices  21.6 us (3%)
  between operations  16.2 us (2%)
    psum x1, blocking collectives, body(): loss_total = lax.psum(local_loss, ('dp', 'expert'))  152 us
    psum x2, waiting for transfers between devices, body(): router_total = lax.psum(lax.psum(router_part, 'expert'), axis_name='dp')  105 us
    all_to_all x1, blocking collectives, body(): lax.all_to_all(outgoing, 'expert', split_axis=0, concat_axis=1, tiled=True)  71.7 us
    all_to_all x1, waiting for transfers between devices, body(): lax.all_to_all(sending, 'expert', split_axis=0, concat_axis=1, tiled=True)  64.7 us
    all_to_all x1, waiting for transfers between devices, body(): lax.all_to_all(result, 'expert', split_axis=1, concat_axis=0, tiled=True)  55.4 us
    scatter-add x1, other arithmetic, body(): added = jnp.zeros((token_count, model_width), jnp.float32).at[flat_index]...  25.3 us
    dot_general x2, matrix products, input_term(): jnp.einsum('jsrd,jsrf->djf', arrived, grads_in, preferred_element_type=jn...  22.1 us
    unnamed x47, local copies, waits for them, and re-layouts  20.9 us
  transfers between devices with their start and end apart: 7, of which 4 were waited for; matrix products, arithmetic and copies ran while one was open for 11% of the time, Pallas kernels for 0%

profile of v1, /device:TPU:1, one launch (start us, length us, event | category | flops | bytes accessed | tf_op | source)
XLA Modules:
  0.0 661.4 jit_solution(14163249834587271281)
XLA Ops:
  8.9 12.7 %gather_fusion = bf16[1280,2048]{1,0:T(8,128)(2,1)} fusion(bf16[512,2048]{1,0:T(8,128)(2,1)} %param.9, s32[2048]{0:T(1024)S(1)} %pad_clamp_fusion), kind=kCustom, calls=%fused_computation | custom fusion | bytes 10490880 | tf_op jit(solution)/shard_map/gather | solution.py:18
  21.6 71.7 %all_to_all.45 = bf16[32,1,40,2048]{3,2,1,0:T(8,128)(2,1)S(1)} all-to-all(bf16[32,1,40,2048]{3,2,1,0:T(8,128)(2,1)} %bitcast.90), channel_id=1, replica_groups=mesh['dp'=8,'expert'=16] {'expert'}, dimensions={0} | all-to-all | bytes 10485760 | tf_op jit(solution)/shard_map/all_to_all | solution.py:19
  93.3 4.4 fusion.6
  97.7 6.5 multiply_convert_fusion.3
  104.2 7.7 %fusion.20 = bf16[2,16,40,2048]{3,2,1,0:T(8,128)(2,1)S(1)} fusion(bf16[2,16,40,768]{3,2,1,0:T(8,128)(2,1)} %get-tuple-element.36, bf16[2048,2,768,1]{2,1,0,3:T(2,128)(2,1)} %bitcast.100), kind=kOutput, calls=%fused_computation.34 | convolution fusion | flops 4029153280 | bytes 13500416 | tf_op jit(solution)/shard_map/jsrf,djf->jsrd/dot_general | solution.py:23
  114.6 6.3 all-to-all-start.1
  124.6 10.1 %gather_fusion.2 = f32[1280]{0:T(1024)S(1)} fusion(f32[32,512]{1,0:T(8,128)S(1)} %fusion.36, s32[1280]{0:T(1024)S(1)} %reshape.165), kind=kCustom, calls=%fused_computation.2 | custom fusion | bytes 20480 | tf_op jit(solution)/shard_map/jit(take_along_axis)/gather | solution.py:17
  134.9 55.4 %all-to-all-done.1 = bf16[2,16,40,2048]{3,2,0,1:T(8,128)(2,1)} async-done(((bf16[2,16,40,2048]{3,2,0,1:T(8,128)(2,1)}), bf16[2,16,40,2048]{3,2,0,1:T(8,128)(2,1)}, u32[]{:S(2)}, u32[]{:S(2)}) %all-to-all-start.1) | async-done | bytes 5242912 | tf_op jit(solution)/shard_map/all_to_all | solution.py:26
  190.2 3.9 bitcast_convert_fusion.3
  194.1 4.7 bitcast_multiply_fusion
  198.9 25.3 %scatter_fusion = f32[512,2048]{1,0:T(8,128)} fusion(f32[512,2048]{1,0:T(8,128)} %convert_element_type.66, s32[1280]{0:T(1024)S(1)} %fusion.33, f32[1280,2048]{1,0:T(8,128)} %bitcast_multiply_fusion), kind=kCustom, calls=%fused_computation.3 | custom fusion | flops 2621440 | bytes 31462400 | tf_op jit(solution)/shard_map/scatter-add | solution.py:40
  224.2 3.6 multiply_reduce_fusion
  231.5 13.0 %gather_fusion.1 = f32[1280,2048]{1,0:T(8,128)} fusion(f32[512,2048]{1,0:T(8,128)} %fusion.28, s32[2048]{0:T(1024)S(1)} %pad_clamp_fusion), kind=kCustom, calls=%fused_computation.1 | custom fusion | bytes 20976640 | tf_op jit(solution)/shard_map/gather | solution.py:54
  244.5 6.7 %fusion = f32[16,2,40]{2,1,0:T(2,128)S(1)} fusion(f32[16,2,1,40,2048]{4,3,1,0,2:T(8,128)} %bitcast.88, bf16[2,16,40,2048]{3,2,0,1:T(8,128)(2,1)} %all-to-all-done.1), kind=kLoop, calls=%fused_computation.10 | loop fusion | flops 7863040 | bytes 15733760 | tf_op jit(solution)/shard_map/reduce_sum | solution.py:55
  255.9 14.8 %all-to-all-start.2 = ((bf16[32,1,40,2048]{3,2,1,0:T(8,128)(2,1)}), bf16[32,1,40,2048]{3,2,1,0:T(8,128)(2,1)}, u32[]{:S(2)}, u32[]{:S(2)}) async-start(bf16[32,1,40,2048]{3,2,1,0:T(8,128)(2,1)} %multiply_convert_fusion), calls=%async_computation.2 | async-start | bytes 10485760 | tf_op jit(solution)/shard_map/all_to_all | solution.py:67
  271.1 5.3 scatter_custom_fusion.1
  278.3 64.7 %all-to-all-done.2 = bf16[32,1,40,2048]{3,2,1,0:T(8,128)(2,1)} async-done(((bf16[32,1,40,2048]{3,2,1,0:T(8,128)(2,1)}), bf16[32,1,40,2048]{3,2,1,0:T(8,128)(2,1)}, u32[]{:S(2)}, u32[]{:S(2)}) %all-to-all-start.2) | async-done | bytes 5242912 | tf_op jit(solution)/shard_map/all_to_all | solution.py:67
  343.0 9.8 %fusion.3 = bf16[2048,2,768]{0,2,1:T(8,128)(2,1)} fusion(bf16[2,16,40,768]{3,2,1,0:T(8,128)(2,1)} %get-tuple-element.36, bf16[16,2,1,40,2048]{4,3,1,0,2:T(8,128)(2,1)} %bitcast.20), kind=kOutput, calls=%fused_computation.14 | convolution fusion | flops 4029677568 | bytes 13500416 | tf_op jit(solution)/shard_map/jsrd,jsrf->djf/dot_general | solution.py:87
  353.1 8.2 %fusion.8 = f32[2,16,40,768]{3,2,1,0:T(8,128)S(1)} fusion(bf16[2048,2,768,1]{2,1,0,3:T(2,128)(2,1)} %bitcast.101, bf16[16,2,1,40,2048]{4,3,1,0,2:T(8,128)(2,1)} %bitcast.20), kind=kOutput, calls=%fused_computation.19 | convolution fusion | flops 4026531840 | bytes 15466496 | tf_op jit(solution)/shard_map/jsrd,djf->jsrf/dot_general | solution.py:68
  363.3 9.9 %fusion.2 = bf16[2048,2,768]{0,2,1:T(8,128)(2,1)} fusion(bf16[16,2,1,40,2048]{4,3,1,0,2:T(8,128)(2,1)} %bitcast.93, f32[2,16,40,768]{3,2,1,0:T(8,128)S(1)} %fusion.8, f32[2,16,40,768]{3,2,1,0:T(8,128)S(1)} %copy-done.16), kind=kOutput, calls=%fused_computation.13 | convolution fusion | flops 4035575808 | bytes 19398656 | tf_op jit(solution)/shard_map/jsrd,jsrf->djf/dot_general | solution.py:78
  373.3 12.3 %fusion.1 = bf16[2048,2,768]{0,2,1:T(8,128)(2,1)} fusion(bf16[16,2,1,40,2048]{4,3,1,0,2:T(8,128)(2,1)} %bitcast.94, f32[2,16,40,768]{3,2,1,0:T(8,128)} %copy-done.15, f32[2,16,40,768]{3,2,1,0:T(8,128)} %copy-done.17, f32[2,16,40,768]{3,2,1,0:T(8,128)} %get-tuple-element.37), kind=kOutput, calls=%fused_computation.12 | convolution fusion | flops 4039507968 | bytes 23330816 | tf_op jit(solution)/shard_map/jsrd,jsrf->djf/dot_general | solution.py:78
  385.6 91.3 %all-reduce.3.cloned.1.call-done = f32[2048,32]{0,1:T(8,128)} async-done(((f32[2048,32]{0,1:T(8,128)}), f32[2048,32]{0,1:T(8,128)}) %all-reduce.3.cloned.1.call-update) | async-done | bytes 262160 | tf_op jit(solution)/shard_map/psum | solution.py:94
  476.9 151.6 %psum.21 = f32[22]{0:T(128)S(1)} all-reduce(f32[22]{0:T(128)S(1)} %get-tuple-element.31), channel_id=1, replica_groups=mesh['dp'=8,'expert'=16] {'dp','expert'}, use_global_device_ids=true, to_apply=%region_3.4 | all-reduce | flops 22 | bytes 176 | tf_op jit(solution)/shard_map/psum | solution.py:49
  638.1 13.8 %all-reduce.5.cloned.1.call-done = f32[2048,32]{0,1:T(8,128)} async-done(((f32[2048,32]{0,1:T(8,128)}), f32[2048,32]{0,1:T(8,128)}) %all-reduce.5.cloned.1.call-update) | async-done | bytes 262160 | tf_op jit(solution)/shard_map/psum | solution.py:94
  (84 shorter events, 31.6 us)
Async XLA Ops:
  8.0 115.9 %copy-start = (bf16[2048,32]{0,1:T(8,128)(2,1)S(1)}, bf16[2048,32]{0,1:T(8,128)(2,1)}, u32[]{:S(2)}) copy-start(bf16[2048,32]{0,1:T(8,128)(2,1)} %param.13) | copy-start | bytes 393220
  8.8 12.8 %copy-start.8 = (s32[32,40,1]{1,0,2:T(8,128)}, s32[32,40,1]{1,0,2:T(8,128)S(1)}, u32[]{:S(2)}) copy-start(s32[32,40,1]{1,0,2:T(8,128)S(1)} %get-tuple-element.35) | copy-start | bytes 15364
  21.6 71.7 %copy-start.14 = (bf16[2048,2,768]{2,1,0:T(2,128)(2,1)S(1)}, bf16[2048,2,768]{2,1,0:T(2,128)(2,1)}, u32[]{:S(2)}) copy-start(bf16[2048,2,768]{2,1,0:T(2,128)(2,1)} %param.15) | copy-start | bytes 18874372
  21.6 76.1 %slice-start = ((s8[6291456]{0:T(1024)(128)(4,1)}), s8[4194304]{0:T(1024)(128)(4,1)S(1)}, s32[]{:S(2)}) async-start(s8[6291456]{0:T(1024)(128)(4,1)} %bitcast.97), calls=%async_computation.11 | async-start | bytes 8388608
  93.3 4.4 copy-start.6
  93.3 4.4 slice-start.1
  97.6 6.6 copy-start.15
  114.6 6.3 copy-start.7
  114.6 6.4 copy-start.3
  114.6 75.6 %all-to-all-start.1 = ((bf16[2,16,40,2048]{3,2,0,1:T(8,128)(2,1)}), bf16[2,16,40,2048]{3,2,0,1:T(8,128)(2,1)}, u32[]{:S(2)}, u32[]{:S(2)}) async-start(bf16[2,16,40,2048]{3,2,0,1:T(8,128)(2,1)} %copy.64), calls=%async_computation.1 | async-start | bytes 10485760 | tf_op jit(solution)/shard_map/all_to_all | solution.py:26
  198.9 29.0 %copy-start.13 = (f32[22]{0:T(128)S(1)}, f32[22]{0:T(128)}, u32[]{:S(2)}) copy-start(f32[22]{0:T(128)} %param.12) | copy-start | bytes 268
  224.2 4.7 copy-start.5
  244.5 8.5 %copy-start.4 = (f32[1280,2048]{1,0:T(8,128)S(1)}, f32[1280,2048]{1,0:T(8,128)}, u32[]{:S(2)}) copy-start(f32[1280,2048]{1,0:T(8,128)} %gather_fusion.1) | copy-start | bytes 31457284
  255.9 14.9 %copy-start.9 = (s32[32,40,1]{1,0,2:T(8,128)S(1)}, s32[32,40,1]{1,0,2:T(8,128)}, u32[]{:S(2)}) copy-start(s32[32,40,1]{1,0,2:T(8,128)} %copy-done.8) | copy-start | bytes 15364
  255.9 14.9 %copy-start.11 = (s32[2]{0:T(128)S(1)}, s32[2]{0:T(128)}, u32[]{:S(2)}) copy-start(s32[2]{0:T(128)} %constant.42) | copy-start | bytes 28
  255.9 15.0 %copy-start.12 = (s32[2]{0:T(128)S(1)}, s32[2]{0:T(128)}, u32[]{:S(2)}) copy-start(s32[2]{0:T(128)} %constant.45) | copy-start | bytes 28
  255.9 87.1 %all-to-all-start.2 = ((bf16[32,1,40,2048]{3,2,1,0:T(8,128)(2,1)}), bf16[32,1,40,2048]{3,2,1,0:T(8,128)(2,1)}, u32[]{:S(2)}, u32[]{:S(2)}) async-start(bf16[32,1,40,2048]{3,2,1,0:T(8,128)(2,1)} %multiply_convert_fusion), calls=%async_computation.2 | async-start | bytes 10485760 | tf_op jit(solution)/shard_map/all_to_all | solution.py:67
  270.7 206.2 %all-reduce.3.cloned.1.call-start = ((), (), s32[]{:S(2)}) async-start(), calls=%async_computation.6 | async-start | bytes 524288 | tf_op jit(solution)/shard_map/psum | solution.py:94
  278.3 350.8 %reduce-scatter.8.cloned.1.call-start = ((), (), s32[]{:S(2)}) async-start(), calls=%async_computation.10 | async-start | bytes 7077888 | tf_op jit(solution)/shard_map/reduce_scatter | solution.py:86
  352.9 279.2 %reduce-scatter.6.cloned.1.call-start = ((), (), s32[]{:S(2)}) async-start(), calls=%async_computation.9 | async-start | bytes 7077888 | tf_op jit(solution)/shard_map/reduce_scatter | solution.py:83
  353.1 10.2 %copy-start.16 = (f32[2,16,40,768]{3,2,1,0:T(8,128)S(1)}, f32[2,16,40,768]{3,2,1,0:T(8,128)}, u32[]{:S(2)}) copy-start(f32[2,16,40,768]{3,2,1,0:T(8,128)} %copy-done.15) | copy-start | bytes 11796484
  373.2 261.9 %reduce-scatter.4.cloned.1.call-start = ((), (), s32[]{:S(2)}) async-start(), calls=%async_computation.8 | async-start | bytes 7077888 | tf_op jit(solution)/shard_map/reduce_scatter | solution.py:80
  385.5 268.0 %copy-start.1 = (bf16[2048,32]{0,1:T(8,128)(2,1)S(1)}, bf16[2048,32]{0,1:T(8,128)(2,1)}, u32[]{:S(2)}) copy-start(bf16[2048,32]{0,1:T(8,128)(2,1)} %param.13) | copy-start | bytes 393220
  385.6 266.3 %all-reduce.5.cloned.1.call-start = ((), (), s32[]{:S(2)}) async-start(), calls=%async_computation.7 | async-start | bytes 524288 | tf_op jit(solution)/shard_map/psum | solution.py:94
  (3 other events, 9.7 us)
Sparse Core Ops, SparseCore 0:
  278.4 198.4 all-reduce.2
Sparse Core Ops, SparseCore 1:
  352.9 80.5 reduce-scatter.7
  435.8 71.5 reduce-scatter.5
  509.7 71.8 reduce-scatter.3
  584.1 67.7 all-reduce.4
